TPU v7x, 32 devices: a whole 2x2x4 slice. The times are simulated.
32 devices in a mesh: left: 8 (over y, x, core), right: 4 (over z).
Axes of the slice: x: 2, y: 2, z: 4, core: 2. Of those that a mesh axis runs over, the one named last changes fastest.
Arguments:
- left_freq: float32 [16384], P('left'), as said below
- right_freq: float32 [16384], P('right'), as said below
- left_dirs: float32 [16, 16384], P(None, 'left'), may hold values from -6 to 6
- left_data: float32 [16, 16384], P(None, 'left'), may hold values from -6 to 6
- right_dirs: float32 [16, 16384], P(None, 'right'), may hold values from -6 to 6
- right_data: float32 [16, 16384], P(None, 'right'), may hold values from -6 to 6
- col_sketch: bfloat16 [16384, 256], P('right'), may hold values from -0.047265625 to 0.047265625
- row_sketch: bfloat16 [16384, 256], P('left'), may hold values from -0.047265625 to 0.047265625
Outputs:
- row_scaled: float32 [16384, 256], P(('left', 'right'))
- col_scaled: float32 [16384, 256], P('right')
- lower_reduced: float32 [256, 256], replicated
- shifted_reduced: float32 [256, 256], replicated
Inputs may be any that keep to these rules, and one draw needn't show every extreme that they name: left_freq[i] = 1 + (k + e) / 16384 with k distinct whole numbers of 0 to 16383 and |e| at most 0.2. right_freq[j] = 1 + (k + 0.5 + e) / 16384 with k distinct whole numbers of 0 to 16383 and |e| at most 0.2; left and right frequencies share the spacing 1 / 16384, so every left and right frequency differ by 0.1 / 16384 or more.
All inputs are finite; a program needn't handle non-finite values.
Results may differ from a plain program's by a relative error of at most 0.0089.
Values sent between devices are 32-bit elements; how exact they have to be, the bound alone decides.
A program may use at most 256 MiB of HBM per device.

v0:
```python
import math
import jax
import jax.numpy as jnp
from jax import lax
from jax.sharding import PartitionSpec as P

precise = lax.Precision.HIGHEST


def build_tiles(freq_rows, dirs_rows, data_rows, right_freq, right_dirs, right_data, total_rows):
    direct = lax.dot_general(
        data_rows,
        right_dirs,
        (((0,), (0,)), ((), ())),
        precision=precise,
        preferred_element_type=jnp.float32,
    )
    crossed = lax.dot_general(
        dirs_rows,
        right_data,
        (((0,), (0,)), ((), ())),
        precision=precise,
        preferred_element_type=jnp.float32,
    )
    spacing_gap = total_rows * (freq_rows[:, None] - right_freq[None, :])
    lower_tile = ((direct - crossed) / spacing_gap).astype(jnp.bfloat16)
    shift_tile = (
        (freq_rows[:, None] * direct - right_freq[None, :] * crossed) / spacing_gap
    ).astype(jnp.bfloat16)
    return (lower_tile, shift_tile)


def gram_of(basis):
    return lax.dot_general(
        basis,
        basis,
        (((0,), (0,)), ((), ())),
        precision=precise,
        preferred_element_type=jnp.float32,
    )


def apply_factor(basis, gram_sum, shifted_flag):
    width = gram_sum.shape[0]
    identity = jnp.eye(width, dtype=jnp.float32)
    if shifted_flag:
        gram_sum = gram_sum + 1e-05 * jnp.trace(gram_sum) / width * identity
    factor = jnp.linalg.cholesky(gram_sum)
    inverse = jax.scipy.linalg.solve_triangular(factor, identity, lower=True)
    return lax.dot_general(
        basis,
        inverse,
        (((1,), (1,)), ((), ())),
        precision=precise,
        preferred_element_type=jnp.float32,
    )


def body(
    left_freq, right_freq, left_dirs, left_data, right_dirs, right_data, col_sketch, row_sketch
):
    row_count = left_freq.shape[0]
    col_count = right_freq.shape[0]
    total_rows = row_count * lax.axis_size("left")
    total_cols = col_count * lax.axis_size("right")
    lower_tile, shift_tile = build_tiles(
        left_freq, left_dirs, left_data, right_freq, right_dirs, right_data, total_rows
    )
    row_image = lax.psum(
        jnp.dot(lower_tile, col_sketch, preferred_element_type=jnp.float32), "right"
    )
    col_image = lax.psum(
        lax.dot_general(
            lower_tile, row_sketch, (((0,), (0,)), ((), ())), preferred_element_type=jnp.float32
        ),
        "left",
    )
    row_full, col_full = (row_image, col_image)
    for sweep_index in range(2):
        gram_rows = lax.psum(gram_of(row_full), "left")
        gram_cols = lax.psum(gram_of(col_full), "right")
        row_full = apply_factor(row_full, gram_rows, sweep_index == 0)
        col_full = apply_factor(col_full, gram_cols, sweep_index == 0)
    share_rows = row_count // lax.axis_size("right")
    row_part = lax.dynamic_slice_in_dim(
        row_full, lax.axis_index("right") * share_rows, share_rows, 0
    )
    col_round = col_full.astype(jnp.bfloat16)
    lower_applied = jnp.dot(lower_tile, col_round, preferred_element_type=jnp.float32)
    shift_applied = jnp.dot(shift_tile, col_round, preferred_element_type=jnp.float32)
    lower_part = lax.dot_general(
        row_full,
        lower_applied,
        (((0,), (0,)), ((), ())),
        precision=precise,
        preferred_element_type=jnp.float32,
    )
    shift_part = lax.dot_general(
        row_full,
        shift_applied,
        (((0,), (0,)), ((), ())),
        precision=precise,
        preferred_element_type=jnp.float32,
    )
    lower_reduced, shifted_reduced = lax.psum((lower_part, shift_part), ("left", "right"))
    return (
        row_part * math.sqrt(total_rows),
        col_full * math.sqrt(total_cols),
        lower_reduced,
        shifted_reduced,
    )


def solution(mesh):
    in_specs = (
        P("left"),
        P("right"),
        P(None, "left"),
        P(None, "left"),
        P(None, "right"),
        P(None, "right"),
        P("right", None),
        P("left", None),
    )
    out_specs = (P(("left", "right"), None), P("right", None), P(), P())
    return jax.shard_map(body, mesh=mesh, in_specs=in_specs, out_specs=out_specs, check_vma=False)
```

profile of v0, /device:TPU:0, one launch (start us, length us, event | category | flops | bytes accessed | tf_op | source)
XLA Modules:
  0.0 872.8 jit_solution(7962259193701451676)
XLA Ops:
  7.3 31.2 %fusion.62 = f32[2048,4096]{1,0:T(8,128)} fusion(f32[16,2048]{1,0:T(8,128)} %param.13, f32[16,4096]{1,0:T(8,128)} %param.16), kind=kOutput, calls=%fused_computation.136 | convolution fusion | flops 1610612736 | bytes 33947648 | tf_op jit(solution)/shard_map/dot_general | solution.py:18
  38.5 40.1 %divide_convert_fusion.1 = (bf16[2048,4096]{1,0:T(8,128)(2,1)}, f32[2048,4096]{1,0:T(8,128)}) fusion(f32[2048,4096]{1,0:T(8,128)} %fusion.62, f32[4096]{0:T(1024)S(1)} %copy-done.8, f32[2048]{0:T(1024)S(1)} %copy-done.9, f32[16,2048]{1,0:T(8,128)S(1)} %copy-done.7, f32[16,4096]{1,0:T(8,128)S(1)} %copy-done.6), kind=kOutput, calls=%fused_computation.9 | convolution fusion | flops 1652555776 | bytes 84303872 | tf_op jit(solution)/shard_map/dot_general | solution.py:11
  88.3 10.5 %fusion.66 = f32[4096,256]{1,0:T(8,128)} fusion(bf16[2048,4096]{1,0:T(8,128)(2,1)} %get-tuple-element.96, bf16[2048,256]{1,0:T(8,128)(2,1)S(1)} %copy-done.5), kind=kOutput, calls=%fused_computation.140 | convolution fusion | flops 4294967296 | bytes 22020096 | tf_op jit(solution)/shard_map/dot_general | solution.py:73
  98.8 78.8 %all-reduce.10.cloned.1.call-done = f32[2048,256]{1,0:T(8,128)} async-done(((f32[2048,256]{1,0:T(8,128)}), f32[2048,256]{1,0:T(8,128)}) %all-reduce.10.cloned.1.call-update) | async-done | bytes 2097168 | tf_op jit(solution)/shard_map/psum | solution.py:69
  184.3 52.3 %all-reduce.12.cloned.1.call-done = f32[256,256]{0,1:T(8,128)} async-done(((f32[256,256]{0,1:T(8,128)}), f32[256,256]{0,1:T(8,128)}) %all-reduce.12.cloned.1.call-update) | async-done | bytes 262160 | tf_op jit(solution)/shard_map/psum | solution.py:80
  241.0 11.7 %cholesky.214 = f32[128,128]{1,0:T(8,128)S(1)} custom-call(f32[128,128]{1,0:T(8,128)S(1)} %cholesky.346), custom_call_target="Cholesky" | custom-call | tf_op jit(solution)/shard_map/jit(cholesky)/cholesky | solution.py:48
  252.7 9.8 %custom-call.17 = f32[1,128,128]{1,2,0:T(8,128)S(1)} custom-call(f32[1,128,128]{2,1,0:T(8,128)S(1)} %get-tuple-element.95), custom_call_target="InvertDiagBlocksLowerTriangular" | custom-call | tf_op jit(solution)/shard_map/jit(cholesky)/cholesky | solution.py:48
  263.1 11.7 %cholesky.231 = f32[128,128]{1,0:T(8,128)S(1)} custom-call(f32[128,128]{1,0:T(8,128)S(1)} %convolution_subtract_fusion.7), custom_call_target="Cholesky" | custom-call | tf_op jit(solution)/shard_map/jit(cholesky)/cholesky | solution.py:48
  281.1 19.7 %custom-call.18 = f32[2,128,128]{1,2,0:T(8,128)S(1)} custom-call(f32[2,128,128]{2,1,0:T(8,128)S(1)} %get-tuple-element.32), custom_call_target="InvertDiagBlocksLowerTriangular" | custom-call | tf_op jit(solution)/shard_map/jit(_solve_triangular)/triangular_solve | solution.py:49
  310.0 83.1 %all-reduce.20.cloned.1.call-done = (f32[256,256]{0,1:T(8,128)}, f32[4096,256]{1,0:T(8,128)}) async-done(((f32[256,256]{0,1:T(8,128)}, f32[4096,256]{1,0:T(8,128)}), (f32[256,256]{0,1:T(8,128)}, f32[4096,256]{1,0:T(8,128)})) %all-reduce.20.cloned.1.call-update) | async-done | bytes 4456464 | tf_op jit(solution)/shard_map/psum | solution.py:80
  395.2 11.7 %cholesky.248 = f32[128,128]{1,0:T(8,128)S(1)} custom-call(f32[128,128]{1,0:T(8,128)S(1)} %cholesky.349), custom_call_target="Cholesky" | custom-call | tf_op jit(solution)/shard_map/jit(cholesky)/cholesky | solution.py:48
  417.9 11.7 %cholesky.265 = f32[128,128]{1,0:T(8,128)S(1)} custom-call(f32[128,128]{1,0:T(8,128)S(1)} %convolution_subtract_fusion.6), custom_call_target="Cholesky" | custom-call | tf_op jit(solution)/shard_map/jit(cholesky)/cholesky | solution.py:48
  435.9 19.7 %custom-call.20 = f32[2,128,128]{1,2,0:T(8,128)S(1)} custom-call(f32[2,128,128]{2,1,0:T(8,128)S(1)} %get-tuple-element.33), custom_call_target="InvertDiagBlocksLowerTriangular" | custom-call | tf_op jit(solution)/shard_map/jit(_solve_triangular)/triangular_solve | solution.py:49
  455.9 10.9 %fusion.67 = f32[256,256]{0,1:T(8,128)} fusion(f32[4096,256]{1,0:T(8,128)} %get-tuple-element.71), kind=kOutput, calls=%fused_computation.141 | convolution fusion | flops 3221225472 | bytes 4456448 | tf_op jit(solution)/shard_map/dot_general | solution.py:34
  467.8 34.5 %all-reduce.14.cloned.1.call-done = f32[256,256]{0,1:T(8,128)} async-done(((f32[256,256]{0,1:T(8,128)}), f32[256,256]{0,1:T(8,128)}) %all-reduce.14.cloned.1.call-update) | async-done | bytes 262160 | tf_op jit(solution)/shard_map/psum | solution.py:81
  506.7 11.7 %cholesky.282 = f32[128,128]{1,0:T(8,128)S(1)} custom-call(f32[128,128]{1,0:T(8,128)S(1)} %cholesky.352), custom_call_target="Cholesky" | custom-call | tf_op jit(solution)/shard_map/jit(cholesky)/cholesky | solution.py:48
  529.4 11.7 %cholesky.299 = f32[128,128]{1,0:T(8,128)S(1)} custom-call(f32[128,128]{1,0:T(8,128)S(1)} %convolution_subtract_fusion.5), custom_call_target="Cholesky" | custom-call | tf_op jit(solution)/shard_map/jit(cholesky)/cholesky | solution.py:48
  547.5 19.7 %custom-call.22 = f32[2,128,128]{1,2,0:T(8,128)S(1)} custom-call(f32[2,128,128]{2,1,0:T(8,128)S(1)} %get-tuple-element.34), custom_call_target="InvertDiagBlocksLowerTriangular" | custom-call | tf_op jit(solution)/shard_map/jit(_solve_triangular)/triangular_solve | solution.py:49
  586.4 31.8 %all-reduce.16.cloned.1.call-done = f32[256,256]{0,1:T(8,128)} async-done(((f32[256,256]{0,1:T(8,128)}), f32[256,256]{0,1:T(8,128)}) %all-reduce.16.cloned.1.call-update) | async-done | bytes 262160 | tf_op jit(solution)/shard_map/psum | solution.py:81
  620.3 11.7 %cholesky.316 = f32[128,128]{1,0:T(8,128)S(1)} custom-call(f32[128,128]{1,0:T(8,128)S(1)} %cholesky.355), custom_call_target="Cholesky" | custom-call | tf_op jit(solution)/shard_map/jit(cholesky)/cholesky | solution.py:48
  643.0 11.9 %cholesky.333 = f32[128,128]{1,0:T(8,128)S(1)} custom-call(f32[128,128]{1,0:T(8,128)S(1)} %convolution_subtract_fusion.4), custom_call_target="Cholesky" | custom-call | tf_op jit(solution)/shard_map/jit(cholesky)/cholesky | solution.py:48
  660.9 19.7 %custom-call.24 = f32[2,128,128]{1,2,0:T(8,128)S(1)} custom-call(f32[2,128,128]{2,1,0:T(8,128)S(1)} %get-tuple-element.35), custom_call_target="InvertDiagBlocksLowerTriangular" | custom-call | tf_op jit(solution)/shard_map/jit(_solve_triangular)/triangular_solve | solution.py:49
  698.8 24.5 %fusion = f32[2048,256]{1,0:T(8,128)} fusion(f32[2048,4096]{1,0:T(8,128)} %fusion.62, f32[2048,4096]{1,0:T(8,128)} %get-tuple-element.97, f32[4096]{0:T(1024)S(1)} %copy-done.8, f32[2048]{0:T(1024)S(1)} %copy-done.9, bf16[4096,256]{1,0:T(8,128)(2,1)S(1)} %get-tuple-element.107), kind=kOutput, calls=%fused_computation.11 | convolution fusion | flops 4353687552 | bytes 71327744 | tf_op jit(solution)/shard_map/dot_general | solution.py:90
  736.1 126.1 %all-reduce.18.cloned.1.call-done = (f32[256,256]{1,0:T(8,128)}, f32[256,256]{1,0:T(8,128)}) async-done(((f32[256,256]{1,0:T(8,128)}, f32[256,256]{1,0:T(8,128)}), (f32[256,256]{1,0:T(8,128)}, f32[256,256]{1,0:T(8,128)})) %all-reduce.18.cloned.1.call-update) | async-done | bytes 524304 | tf_op jit(solution)/shard_map/psum | solution.py:105
  (143 shorter events, 160.6 us)
Async XLA Ops:
  7.2 71.5 %copy-start = (bf16[4096,256]{1,0:T(8,128)(2,1)S(1)}, bf16[4096,256]{1,0:T(8,128)(2,1)}, u32[]{:S(2)}) copy-start(bf16[4096,256]{1,0:T(8,128)(2,1)} %param.17) | copy-start | bytes 6291460
  7.2 31.3 %copy-start.8 = (f32[4096]{0:T(1024)S(1)}, f32[4096]{0:T(1024)}, u32[]{:S(2)}) copy-start(f32[4096]{0:T(1024)} %param.12) | copy-start | bytes 49156
  7.2 31.3 %copy-start.9 = (f32[2048]{0:T(1024)S(1)}, f32[2048]{0:T(1024)}, u32[]{:S(2)}) copy-start(f32[2048]{0:T(1024)} %param.11) | copy-start | bytes 24580
  7.2 31.3 %copy-start.6 = (f32[16,4096]{1,0:T(8,128)S(1)}, f32[16,4096]{1,0:T(8,128)}, u32[]{:S(2)}) copy-start(f32[16,4096]{1,0:T(8,128)} %param.15) | copy-start | bytes 786436
  7.2 31.3 %copy-start.7 = (f32[16,2048]{1,0:T(8,128)S(1)}, f32[16,2048]{1,0:T(8,128)}, u32[]{:S(2)}) copy-start(f32[16,2048]{1,0:T(8,128)} %param.14) | copy-start | bytes 393220
  7.2 170.4 %all-reduce.10.cloned.1.call-start = ((), (), s32[]{:S(2)}) async-start(), calls=%async_computation | async-start | bytes 4194304 | tf_op jit(solution)/shard_map/psum | solution.py:69
  78.6 9.6 %copy-start.5 = (bf16[2048,256]{1,0:T(8,128)(2,1)S(1)}, bf16[2048,256]{1,0:T(8,128)(2,1)}, u32[]{:S(2)}) copy-start(bf16[2048,256]{1,0:T(8,128)(2,1)} %param.18) | copy-start | bytes 3145732
  88.2 148.4 %all-reduce.12.cloned.1.call-start = ((), (), s32[]{:S(2)}) async-start(), calls=%async_computation.1 | async-start | bytes 524288 | tf_op jit(solution)/shard_map/psum | solution.py:80
  184.0 209.1 %all-reduce.20.cloned.1.call-start = ((), (), s32[]{:S(2)}) async-start(), calls=%async_computation.5 | async-start | bytes 8912896 | tf_op jit(solution)/shard_map/psum | solution.py:80
  309.5 192.8 %all-reduce.14.cloned.1.call-start = ((), (), s32[]{:S(2)}) async-start(), calls=%async_computation.2 | async-start | bytes 524288 | tf_op jit(solution)/shard_map/psum | solution.py:81
  466.8 151.4 %all-reduce.16.cloned.1.call-start = ((), (), s32[]{:S(2)}) async-start(), calls=%async_computation.3 | async-start | bytes 524288 | tf_op jit(solution)/shard_map/psum | solution.py:81
  573.6 2.0 copy-start.2
  583.0 279.2 %all-reduce.18.cloned.1.call-start = ((), (), s32[]{:S(2)}) async-start(), calls=%async_computation.4 | async-start | bytes 1048576 | tf_op jit(solution)/shard_map/psum | solution.py:105
  723.3 6.6 copy-start.3
  723.3 6.6 copy-start.4
  723.3 142.2 %copy-start.1 = (bf16[4096,256]{1,0:T(8,128)(2,1)S(1)}, bf16[4096,256]{1,0:T(8,128)(2,1)}, u32[]{:S(2)}) copy-start(bf16[4096,256]{1,0:T(8,128)(2,1)} %param.17) | copy-start | bytes 6291460
Sparse Core Ops, SparseCore 0:
  88.3 89.1 all-reduce.9
  184.1 52.4 all-reduce.11
  309.6 83.4 all-reduce.19
  466.9 35.3 all-reduce.13
  583.1 35.0 all-reduce.15
  734.3 127.8 all-reduce.17
where the time goes:
time: 879 us; the launch traced here: 873 us
  waiting for transfers between devices  407 us (46%)
  other arithmetic  228 us (26%)
  matrix products  191 us (22%)
  local copies, waits for them, and re-layouts  23.8 us (3%)
  between operations  21.6 us (2%)
    another operation x27, other arithmetic, apply_factor(): factor = jnp.linalg.cholesky(gram_sum)  138 us
    psum x2, waiting for transfers between devices, body(): gram_rows = lax.psum(gram_of(row_full), 'left')  135 us
    psum x1, waiting for transfers between devices, body(): lax.psum((lower_part, shift_part), ('left', 'right'))  126 us
    psum x1, waiting for transfers between devices, body(): lax.psum(jnp.dot(lower_tile, col_sketch, preferred_element_type=jnp.float...  78.8 us
    another operation x9, other arithmetic, apply_factor(): inverse = jax.scipy.linalg.solve_triangular(factor, identity, lower=True)  78.8 us
    psum x2, waiting for transfers between devices, body(): gram_cols = lax.psum(gram_of(col_full), 'right')  66.4 us
    dot_general x1, matrix products, build_tiles(): lax.dot_general(data_rows, right_dirs, (((0,), (0,)), ((), ())), precisio...  40.1 us
    dot_general x1, matrix products, build_tiles(): lax.dot_general(dirs_rows, right_data, (((0,), (0,)), ((), ())), precisio...  31.2 us
  transfers between devices with their start and end apart: 6, of which 6 were waited for; matrix products, arithmetic and copies ran while one was open for 2% of the time, Pallas kernels for 0%

commit v1 on v0

--- a/solution.py
+++ b/solution.py
@@ -102,7 +102,7 @@
         precision=precise,
         preferred_element_type=jnp.float32,
     )
-    lower_reduced, shifted_reduced = lax.psum((lower_part, shift_part), ("left", "right"))
+    lower_reduced, shifted_reduced = lax.psum(lax.psum((lower_part, shift_part), "right"), "left")
     return (
         row_part * math.sqrt(total_rows),
         col_full * math.sqrt(total_cols),

time: 879 us -> 847 us (0.964)
  waiting for transfers between devices: 407 us -> 375 us
    psum x1 -> x2, waiting for transfers between devices: 126 us -> 94.2 us  [the longest x1 55.9 us: body(): lax.psum(lax.psum((lower_part, shift_part), 'right'), 'left')]
  transfers between devices with their start and end apart: 6 -> 7, of which waited for: 6 -> 7; matrix products, arithmetic and copies ran while one was open for 2% -> 2% of each run, Pallas kernels for 0% -> 0%
where the time goes in v1:
time: 847 us; the launch traced here: 841 us
  waiting for transfers between devices  375 us (44%)
  other arithmetic  228 us (27%)
  matrix products  191 us (23%)
  local copies, waits for them, and re-layouts  23.8 us (3%)
  between operations  21.6 us (3%)
    another operation x27, other arithmetic, apply_factor(): factor = jnp.linalg.cholesky(gram_sum)  138 us
    psum x2, waiting for transfers between devices, body(): gram_rows = lax.psum(gram_of(row_full), 'left')  135 us
    psum x1, waiting for transfers between devices, body(): lax.psum(jnp.dot(lower_tile, col_sketch, preferred_element_type=jnp.float...  78.8 us
    another operation x9, other arithmetic, apply_factor(): inverse = jax.scipy.linalg.solve_triangular(factor, identity, lower=True)  78.8 us
    psum x2, waiting for transfers between devices, body(): gram_cols = lax.psum(gram_of(col_full), 'right')  66.4 us
    psum x1, waiting for transfers between devices, body(): lax.psum(lax.psum((lower_part, shift_part), 'right'), 'left')  55.9 us
    dot_general x1, matrix products, build_tiles(): lax.dot_general(data_rows, right_dirs, (((0,), (0,)), ((), ())), precisio...  40.1 us
    psum x1, waiting for transfers between devices, body(): lax.psum((lower_part, shift_part), 'right')  38.3 us
  transfers between devices with their start and end apart: 7, of which 7 were waited for; matrix products, arithmetic and copies ran while one was open for 2% of the time, Pallas kernels for 0%

profile of v1, /device:TPU:0, one launch (start us, length us, event | category | flops | bytes accessed | tf_op | source)
XLA Modules:
  0.0 841.0 jit_solution(5082906906481345808)
XLA Ops:
  7.3 31.2 %fusion.62 = f32[2048,4096]{1,0:T(8,128)} fusion(f32[16,2048]{1,0:T(8,128)} %param.13, f32[16,4096]{1,0:T(8,128)} %param.16), kind=kOutput, calls=%fused_computation.136 | convolution fusion | flops 1610612736 | bytes 33947648 | tf_op jit(solution)/shard_map/dot_general | solution.py:18
  38.5 40.1 %divide_convert_fusion.1 = (bf16[2048,4096]{1,0:T(8,128)(2,1)}, f32[2048,4096]{1,0:T(8,128)}) fusion(f32[2048,4096]{1,0:T(8,128)} %fusion.62, f32[4096]{0:T(1024)S(1)} %copy-done.8, f32[2048]{0:T(1024)S(1)} %copy-done.9, f32[16,2048]{1,0:T(8,128)S(1)} %copy-done.7, f32[16,4096]{1,0:T(8,128)S(1)} %copy-done.6), kind=kOutput, calls=%fused_computation.9 | convolution fusion | flops 1652555776 | bytes 84303872 | tf_op jit(solution)/shard_map/dot_general | solution.py:11
  88.3 10.5 %fusion.66 = f32[4096,256]{1,0:T(8,128)} fusion(bf16[2048,4096]{1,0:T(8,128)(2,1)} %get-tuple-element.98, bf16[2048,256]{1,0:T(8,128)(2,1)S(1)} %copy-done.5), kind=kOutput, calls=%fused_computation.140 | convolution fusion | flops 4294967296 | bytes 22020096 | tf_op jit(solution)/shard_map/dot_general | solution.py:73
  98.8 78.8 %all-reduce.12.cloned.1.call-done = f32[2048,256]{1,0:T(8,128)} async-done(((f32[2048,256]{1,0:T(8,128)}), f32[2048,256]{1,0:T(8,128)}) %all-reduce.12.cloned.1.call-update) | async-done | bytes 2097168 | tf_op jit(solution)/shard_map/psum | solution.py:69
  184.3 52.3 %all-reduce.14.cloned.1.call-done = f32[256,256]{0,1:T(8,128)} async-done(((f32[256,256]{0,1:T(8,128)}), f32[256,256]{0,1:T(8,128)}) %all-reduce.14.cloned.1.call-update) | async-done | bytes 262160 | tf_op jit(solution)/shard_map/psum | solution.py:80
  241.0 11.7 %cholesky.214 = f32[128,128]{1,0:T(8,128)S(1)} custom-call(f32[128,128]{1,0:T(8,128)S(1)} %cholesky.346), custom_call_target="Cholesky" | custom-call | tf_op jit(solution)/shard_map/jit(cholesky)/cholesky | solution.py:48
  263.1 11.7 %cholesky.231 = f32[128,128]{1,0:T(8,128)S(1)} custom-call(f32[128,128]{1,0:T(8,128)S(1)} %convolution_subtract_fusion.7), custom_call_target="Cholesky" | custom-call | tf_op jit(solution)/shard_map/jit(cholesky)/cholesky | solution.py:48
  281.1 19.7 %custom-call.18 = f32[2,128,128]{1,2,0:T(8,128)S(1)} custom-call(f32[2,128,128]{2,1,0:T(8,128)S(1)} %get-tuple-element.32), custom_call_target="InvertDiagBlocksLowerTriangular" | custom-call | tf_op jit(solution)/shard_map/jit(_solve_triangular)/triangular_solve | solution.py:49
  310.0 83.1 %all-reduce.22.cloned.1.call-done = (f32[256,256]{0,1:T(8,128)}, f32[4096,256]{1,0:T(8,128)}) async-done(((f32[256,256]{0,1:T(8,128)}, f32[4096,256]{1,0:T(8,128)}), (f32[256,256]{0,1:T(8,128)}, f32[4096,256]{1,0:T(8,128)})) %all-reduce.22.cloned.1.call-update) | async-done | bytes 4456464 | tf_op jit(solution)/shard_map/psum | solution.py:80
  395.2 11.7 %cholesky.248 = f32[128,128]{1,0:T(8,128)S(1)} custom-call(f32[128,128]{1,0:T(8,128)S(1)} %cholesky.349), custom_call_target="Cholesky" | custom-call | tf_op jit(solution)/shard_map/jit(cholesky)/cholesky | solution.py:48
  417.9 11.7 %cholesky.265 = f32[128,128]{1,0:T(8,128)S(1)} custom-call(f32[128,128]{1,0:T(8,128)S(1)} %convolution_subtract_fusion.6), custom_call_target="Cholesky" | custom-call | tf_op jit(solution)/shard_map/jit(cholesky)/cholesky | solution.py:48
  435.9 19.7 %custom-call.20 = f32[2,128,128]{1,2,0:T(8,128)S(1)} custom-call(f32[2,128,128]{2,1,0:T(8,128)S(1)} %get-tuple-element.33), custom_call_target="InvertDiagBlocksLowerTriangular" | custom-call | tf_op jit(solution)/shard_map/jit(_solve_triangular)/triangular_solve | solution.py:49
  455.9 10.9 %fusion.67 = f32[256,256]{0,1:T(8,128)} fusion(f32[4096,256]{1,0:T(8,128)} %get-tuple-element.71), kind=kOutput, calls=%fused_computation.141 | convolution fusion | flops 3221225472 | bytes 4456448 | tf_op jit(solution)/shard_map/dot_general | solution.py:34
  467.8 34.5 %all-reduce.16.cloned.1.call-done = f32[256,256]{0,1:T(8,128)} async-done(((f32[256,256]{0,1:T(8,128)}), f32[256,256]{0,1:T(8,128)}) %all-reduce.16.cloned.1.call-update) | async-done | bytes 262160 | tf_op jit(solution)/shard_map/psum | solution.py:81
  506.7 11.7 %cholesky.282 = f32[128,128]{1,0:T(8,128)S(1)} custom-call(f32[128,128]{1,0:T(8,128)S(1)} %cholesky.352), custom_call_target="Cholesky" | custom-call | tf_op jit(solution)/shard_map/jit(cholesky)/cholesky | solution.py:48
  529.4 11.7 %cholesky.299 = f32[128,128]{1,0:T(8,128)S(1)} custom-call(f32[128,128]{1,0:T(8,128)S(1)} %convolution_subtract_fusion.5), custom_call_target="Cholesky" | custom-call | tf_op jit(solution)/shard_map/jit(cholesky)/cholesky | solution.py:48
  547.5 19.7 %custom-call.22 = f32[2,128,128]{1,2,0:T(8,128)S(1)} custom-call(f32[2,128,128]{2,1,0:T(8,128)S(1)} %get-tuple-element.34), custom_call_target="InvertDiagBlocksLowerTriangular" | custom-call | tf_op jit(solution)/shard_map/jit(_solve_triangular)/triangular_solve | solution.py:49
  586.4 31.8 %all-reduce.18.cloned.1.call-done = f32[256,256]{0,1:T(8,128)} async-done(((f32[256,256]{0,1:T(8,128)}), f32[256,256]{0,1:T(8,128)}) %all-reduce.18.cloned.1.call-update) | async-done | bytes 262160 | tf_op jit(solution)/shard_map/psum | solution.py:81
  620.3 11.7 %cholesky.316 = f32[128,128]{1,0:T(8,128)S(1)} custom-call(f32[128,128]{1,0:T(8,128)S(1)} %cholesky.355), custom_call_target="Cholesky" | custom-call | tf_op jit(solution)/shard_map/jit(cholesky)/cholesky | solution.py:48
  643.0 11.9 %cholesky.333 = f32[128,128]{1,0:T(8,128)S(1)} custom-call(f32[128,128]{1,0:T(8,128)S(1)} %convolution_subtract_fusion.4), custom_call_target="Cholesky" | custom-call | tf_op jit(solution)/shard_map/jit(cholesky)/cholesky | solution.py:48
  660.9 19.7 %custom-call.24 = f32[2,128,128]{1,2,0:T(8,128)S(1)} custom-call(f32[2,128,128]{2,1,0:T(8,128)S(1)} %get-tuple-element.35), custom_call_target="InvertDiagBlocksLowerTriangular" | custom-call | tf_op jit(solution)/shard_map/jit(_solve_triangular)/triangular_solve | solution.py:49
  698.8 24.5 %fusion = f32[2048,256]{1,0:T(8,128)} fusion(f32[2048,4096]{1,0:T(8,128)} %fusion.62, f32[2048,4096]{1,0:T(8,128)} %get-tuple-element.99, f32[4096]{0:T(1024)S(1)} %copy-done.8, f32[2048]{0:T(1024)S(1)} %copy-done.9, bf16[4096,256]{1,0:T(8,128)(2,1)S(1)} %get-tuple-element.109), kind=kOutput, calls=%fused_computation.11 | convolution fusion | flops 4353687552 | bytes 71327744 | tf_op jit(solution)/shard_map/dot_general | solution.py:90
  734.2 38.3 %all-reduce.24.cloned.1.call-done = (f32[256,256]{1,0:T(8,128)}, f32[256,256]{1,0:T(8,128)}) async-done(((f32[256,256]{1,0:T(8,128)}, f32[256,256]{1,0:T(8,128)}), (f32[256,256]{1,0:T(8,128)}, f32[256,256]{1,0:T(8,128)})) %all-reduce.24.cloned.1.call-update) | async-done | bytes 524304 | tf_op jit(solution)/shard_map/psum | solution.py:105
  774.5 55.9 %all-reduce.20.cloned.1.call-done = (f32[256,256]{1,0:T(8,128)}, f32[256,256]{1,0:T(8,128)}) async-done(((f32[256,256]{1,0:T(8,128)}, f32[256,256]{1,0:T(8,128)}), (f32[256,256]{1,0:T(8,128)}, f32[256,256]{1,0:T(8,128)})) %all-reduce.20.cloned.1.call-update) | async-done | bytes 524304 | tf_op jit(solution)/shard_map/psum | solution.py:105
  (146 shorter events, 170.5 us)
Async XLA Ops:
  7.2 71.5 %copy-start = (bf16[4096,256]{1,0:T(8,128)(2,1)S(1)}, bf16[4096,256]{1,0:T(8,128)(2,1)}, u32[]{:S(2)}) copy-start(bf16[4096,256]{1,0:T(8,128)(2,1)} %param.17) | copy-start | bytes 6291460
  7.2 31.3 %copy-start.8 = (f32[4096]{0:T(1024)S(1)}, f32[4096]{0:T(1024)}, u32[]{:S(2)}) copy-start(f32[4096]{0:T(1024)} %param.12) | copy-start | bytes 49156
  7.2 31.3 %copy-start.9 = (f32[2048]{0:T(1024)S(1)}, f32[2048]{0:T(1024)}, u32[]{:S(2)}) copy-start(f32[2048]{0:T(1024)} %param.11) | copy-start | bytes 24580
  7.2 31.3 %copy-start.6 = (f32[16,4096]{1,0:T(8,128)S(1)}, f32[16,4096]{1,0:T(8,128)}, u32[]{:S(2)}) copy-start(f32[16,4096]{1,0:T(8,128)} %param.15) | copy-start | bytes 786436
  7.2 31.3 %copy-start.7 = (f32[16,2048]{1,0:T(8,128)S(1)}, f32[16,2048]{1,0:T(8,128)}, u32[]{:S(2)}) copy-start(f32[16,2048]{1,0:T(8,128)} %param.14) | copy-start | bytes 393220
  7.2 170.4 %all-reduce.12.cloned.1.call-start = ((), (), s32[]{:S(2)}) async-start(), calls=%async_computation | async-start | bytes 4194304 | tf_op jit(solution)/shard_map/psum | solution.py:69
  78.6 9.6 %copy-start.5 = (bf16[2048,256]{1,0:T(8,128)(2,1)S(1)}, bf16[2048,256]{1,0:T(8,128)(2,1)}, u32[]{:S(2)}) copy-start(bf16[2048,256]{1,0:T(8,128)(2,1)} %param.18) | copy-start | bytes 3145732
  88.2 148.4 %all-reduce.14.cloned.1.call-start = ((), (), s32[]{:S(2)}) async-start(), calls=%async_computation.1 | async-start | bytes 524288 | tf_op jit(solution)/shard_map/psum | solution.py:80
  184.0 209.1 %all-reduce.22.cloned.1.call-start = ((), (), s32[]{:S(2)}) async-start(), calls=%async_computation.5 | async-start | bytes 8912896 | tf_op jit(solution)/shard_map/psum | solution.py:80
  309.5 192.8 %all-reduce.16.cloned.1.call-start = ((), (), s32[]{:S(2)}) async-start(), calls=%async_computation.2 | async-start | bytes 524288 | tf_op jit(solution)/shard_map/psum | solution.py:81
  466.8 151.4 %all-reduce.18.cloned.1.call-start = ((), (), s32[]{:S(2)}) async-start(), calls=%async_computation.3 | async-start | bytes 524288 | tf_op jit(solution)/shard_map/psum | solution.py:81
  573.6 2.0 copy-start.2
  583.0 189.6 %all-reduce.24.cloned.1.call-start = ((), (), s32[]{:S(2)}) async-start(), calls=%async_computation.6 | async-start | bytes 1048576 | tf_op jit(solution)/shard_map/psum | solution.py:105
  723.3 6.6 copy-start.3
  723.3 6.6 copy-start.4
  723.3 110.4 %copy-start.1 = (bf16[4096,256]{1,0:T(8,128)(2,1)S(1)}, bf16[4096,256]{1,0:T(8,128)(2,1)}, u32[]{:S(2)}) copy-start(bf16[4096,256]{1,0:T(8,128)(2,1)} %param.17) | copy-start | bytes 6291460
  734.2 96.2 %all-reduce.20.cloned.1.call-start = ((), (), s32[]{:S(2)}) async-start(), calls=%async_computation.4 | async-start | bytes 1048576 | tf_op jit(solution)/shard_map/psum | solution.py:105
Sparse Core Ops, SparseCore 0:
  88.3 89.1 all-reduce.11
  184.1 52.4 all-reduce.13
  309.6 83.4 all-reduce.21
  466.9 35.3 all-reduce.15
  583.1 35.0 all-reduce.17
  734.3 38.2 all-reduce.23
  775.7 54.5 all-reduce.19
